TPU v7x, 512 devices: a whole 4x4x16 slice. The times are simulated.
512 devices in a mesh: tm: 64 (over x, z), net: 8 (over y, core).
Axes of the slice: x: 4, y: 4, z: 16, core: 2. Of those that a mesh axis runs over, the one named last changes fastest.
Arguments:
- forcing: float32 [4096, 2, 16384], P('tm', None, 'net'), may hold values from -1.5 to 1.5
- friction_class: int32 [16384], P('net'), may hold values from 0 to 7
- compressor: int32 [16384], P('net'), may hold values 0 or 1
- blocks: float32 [3, 2, 2, 9], replicated, may hold values from -1 to 1, as said below
Outputs:
- solution: float32 [4096, 2, 16384], P('tm', None, 'net')
Inputs may be any that keep to these rules, and one draw needn't show every extreme that they name: `blocks`: each 2 x 2 block has operator norm at most 1.
All inputs are finite; a program needn't handle non-finite values. No bound on the sum of `compressor` on one device may be relied on, other than what follows from the above.
Results may differ from a plain program's by a relative error of at most 0.0003.
Values sent between devices are 32-bit elements; how exact they have to be, the bound alone decides.
No kernel may reach another device: no remote copies, remote signals or barrier semaphores. Data moves between devices by JAX's collectives and lax.ppermute only.
A program may use at most 64 MiB of HBM per device.

v0:
```python
import jax
import jax.numpy as jnp
from jax import lax
from jax.experimental import pallas as pl
from jax.experimental.pallas import tpu as pltpu
from jax.sharding import PartitionSpec as P

FACTOR = 8
KINDS = 9
LANES = 128
TILES = 16
WINDOWS = 64
PACKED = 24
RIGHT = 16
LEFT = 23
EDGE_ROWS = 136
ROWS_OF = list(range(TILES)) + [RIGHT, LEFT]
LISTED = len(ROWS_OF)
PREV = [LISTED - 1] + list(range(TILES)) + [LISTED - 1]
NEXT = list(range(1, TILES + 1)) + [TILES, 0]
SLAB = 32
MARGIN = 48


def lanes_of(shape):
    return lax.broadcasted_iota(jnp.int32, shape, len(shape) - 1)


def couple(p, q, p_low, p_high, q_low, q_high, w):
    mixed_p = (p + p) + (q_high - q_low)
    mixed_q = (q + q) + (p_low - p_high)
    return w[0] * mixed_p + w[1] * mixed_q, w[2] * mixed_p + w[3] * mixed_q


def apply2(p, q, w):
    return w[0] * p + w[1] * q, w[2] * p + w[3] * q


def phi_tiles(ps, qs, weight_of):
    lane = lanes_of((8, LANES))
    first, last = lane == 0, lane == LANES - 1

    def low(xs, t):
        return pltpu.roll(jnp.where(last, xs[PREV[t]], xs[t]), 1, 1)

    def high(xs, t):
        return pltpu.roll(jnp.where(first, xs[NEXT[t]], xs[t]), LANES - 1, 1)

    new_p, new_q = [], []
    for t in range(LISTED):
        p, q = couple(ps[t], qs[t], low(ps, t), high(ps, t), low(qs, t), high(qs, t), weight_of(t))
        new_p.append(p)
        new_q.append(q)
    return new_p, new_q


def phi_packed(p, q, w):
    lane = lanes_of((PACKED, LANES))
    first, last = lane == 0, lane == LANES - 1

    def low(x):
        return pltpu.roll(jnp.where(last, pltpu.roll(x, 1, 0), x), 1, 1)

    def high(x):
        return pltpu.roll(jnp.where(first, pltpu.roll(x, PACKED - 1, 0), x), LANES - 1, 1)

    return couple(p, q, low(p), high(p), low(q), high(q), w)


def phi_slab(p, q, w):
    return couple(
        p, q, pltpu.roll(p, 1, 1), pltpu.roll(p, LANES - 1, 1), pltpu.roll(q, 1, 1), pltpu.roll(q, LANES - 1, 1), w
    )


def pick(blocks_ref, number, kind):
    scale = 1.0 if number == 2 else 0.25
    masks = [kind == float(k + 1) for k in range(KINDS)]
    picked = []
    for entry in range(4):
        chosen = jnp.zeros_like(kind)
        for k in range(KINDS):
            chosen = jnp.where(masks[k], blocks_ref[(number * 4 + entry) * KINDS + k] * scale, chosen)
        picked.append(chosen)
    return picked


def load_forcing(f_ref, right_ref, left_ref, j, t, field):
    if t < TILES:
        return f_ref[pl.ds(j * 32 + t * 2 + field, 8, stride=256), :]
    edge = right_ref if t == TILES else left_ref
    return edge[pl.ds(j * 2 + field, 8, stride=16), :]


def tile_rows(t):
    return pl.ds(ROWS_OF[t] * 8, 8)


def fine_weights(w_ref):
    def weight_of(t):
        return [jnp.broadcast_to(w_ref[e, ROWS_OF[t] : ROWS_OF[t] + 1, :], (8, LANES)) for e in range(4)]

    return weight_of


def first_kernel(blocks_ref, f_ref, right_ref, left_ref, fc_ref, comp_ref, r1_ref, r2_ref, w_ref, kx_ref, send_ref,
                 prev_ref, c_ref, r1b_ref):
    kx_ref[0:TILES, :] = jnp.where(comp_ref[...] == 1, KINDS, fc_ref[...] + 1).astype(jnp.float32)
    kx_ref[TILES:PACKED, :] = jnp.zeros((PACKED - TILES, LANES), jnp.float32)
    kx_ref[RIGHT : RIGHT + 1, :] = right_ref[128:129, :]
    kx_ref[LEFT : LEFT + 1, :] = left_ref[128:129, :]
    kind = kx_ref[...]
    for number in range(3):
        for entry, chosen in enumerate(pick(blocks_ref, number, kind)):
            w_ref[number * 4 + entry] = chosen
    weight_of = fine_weights(w_ref)
    w1 = [w_ref[4 + e] for e in range(4)]

    def forcing(j, field):
        return [load_forcing(f_ref, right_ref, left_ref, j, t, field) for t in range(LISTED)]

    unused = jnp.zeros(((LEFT - RIGHT - 1) * 8, LANES), jnp.float32)
    for field in range(2):
        for ref in (r1_ref, r1b_ref):
            ref[field, (RIGHT + 1) * 8 : LEFT * 8, :] = unused

    ps, qs = forcing(0, 0), forcing(0, 1)
    for j in range(1, FACTOR):
        ps, qs = phi_tiles(ps, qs, weight_of)
        fp, fq = forcing(j, 0), forcing(j, 1)
        ps = [a + b for a, b in zip(ps, fp)]
        qs = [a + b for a, b in zip(qs, fq)]
    for t in range(LISTED):
        r1_ref[0, tile_rows(t), :] = ps[t]
        r1_ref[1, tile_rows(t), :] = qs[t]

    def sweep(ref, keep):
        p = q = None
        for k in range(FACTOR):
            rp, rq = ref[0, pl.ds(k, PACKED, stride=8), :], ref[1, pl.ds(k, PACKED, stride=8), :]
            if k == 0:
                p, q = rp, rq
            else:
                p, q = phi_packed(p, q, w1)
                p, q = p + rp, q + rq
            if keep:
                c_ref[0, pl.ds(k, PACKED, stride=8), :] = p
                c_ref[1, pl.ds(k, PACKED, stride=8), :] = q
                if k < FACTOR - 1:
                    prev_ref[0, pl.ds(k + 1, PACKED, stride=8), :] = p
                    prev_ref[1, pl.ds(k + 1, PACKED, stride=8), :] = q
        return p, q

    nothing = jnp.zeros((PACKED, LANES), jnp.float32)
    prev_ref[0, pl.ds(0, PACKED, stride=8), :] = nothing
    prev_ref[1, pl.ds(0, PACKED, stride=8), :] = nothing
    r2p, r2q = sweep(r1_ref, True)
    r2_ref[0] = r2p
    r2_ref[1] = r2q

    ps = [prev_ref[0, tile_rows(t), :] for t in range(LISTED)]
    qs = [prev_ref[1, tile_rows(t), :] for t in range(LISTED)]
    for j in range(FACTOR):
        ps, qs = phi_tiles(ps, qs, weight_of)
        fp, fq = forcing(j, 0), forcing(j, 1)
        ps = [a + b for a, b in zip(ps, fp)]
        qs = [a + b for a, b in zip(qs, fq)]
    for t in range(LISTED):
        r1b_ref[0, tile_rows(t), :] = ps[t] - c_ref[0, tile_rows(t), :]
        r1b_ref[1, tile_rows(t), :] = qs[t] - c_ref[1, tile_rows(t), :]
    gp, gq = sweep(r1b_ref, False)

    lane = lanes_of((TILES, LANES))
    for c, x in enumerate((r2p, r2q, gp, gq)):
        here, before, after = x[0:TILES], pltpu.roll(x, 1, 0)[0:TILES], pltpu.roll(x, PACKED - 1, 0)[0:TILES]
        for quarter in range(4):
            start = (SLAB * quarter - MARGIN) % LANES
            a, b = (before, here) if quarter < 2 else (here, after)
            piece = pltpu.roll(jnp.where(lane >= start, a, b), LANES - start, 1)
            send_ref[pl.ds(4 * quarter + c, TILES, stride=16), :] = piece


def slab_kernel(place_ref, blocks_ref, kx_ref, got_ref, send_ref, prev_ref, m_ref):
    place = place_ref[0]
    tile, quarter = place // 4, place % 4
    lane = lanes_of((1, LANES))
    start = (quarter * SLAB + (LANES - MARGIN)) % LANES
    base = jnp.where(quarter < 2, tile - 1, tile)
    base = jnp.where(base < 0, LEFT, base)
    after = jnp.where(base == LEFT, 0, base + 1)
    a, b = kx_ref[pl.ds(base, 1), :], kx_ref[pl.ds(after, 1), :]
    kind = pltpu.roll(jnp.where(lane >= start, a, b), LANES - start, 1)
    kind = jnp.broadcast_to(kind, (8, LANES))
    w0, w1, w2 = (pick(blocks_ref, number, kind) for number in range(3))
    sub = lax.broadcasted_iota(jnp.int32, (8, LANES), 0)

    def square(w):
        return [
            w[0] * w[0] + w[1] * w[2],
            w[0] * w[1] + w[1] * w[3],
            w[2] * w[0] + w[3] * w[2],
            w[2] * w[1] + w[3] * w[3],
        ]

    w_eight = square(square(square(w2)))
    w_jump = [w_eight, square(w_eight), square(square(w_eight))]

    def recurrence(rp, rq):
        tp, tq = rp[0], rq[0]
        for b in range(1, 8):
            tp, tq = apply2(tp, tq, w2)
            tp, tq = tp + rp[b], tq + rq[b]
        for step, w in zip((1, 2, 4), w_jump):
            sp = jnp.where(sub >= step, pltpu.roll(tp, step, 0), 0.0)
            sq = jnp.where(sub >= step, pltpu.roll(tq, step, 0), 0.0)
            sp, sq = apply2(sp, sq, w)
            tp, tq = tp + sp, tq + sq
        dp = [jnp.where(sub >= 1, pltpu.roll(tp, 1, 0), 0.0)]
        dq = [jnp.where(sub >= 1, pltpu.roll(tq, 1, 0), 0.0)]
        for b in range(1, 8):
            p, q = apply2(dp[b - 1], dq[b - 1], w2)
            dp.append(p + rp[b - 1])
            dq.append(q + rq[b - 1])
        return dp, dq

    def rows(b, c):
        return pl.ds(b * 4 + c, 8, stride=32)

    dp, dq = recurrence([got_ref[rows(b, 0), :] for b in range(8)], [got_ref[rows(b, 1), :] for b in range(8)])
    zero = jnp.zeros((8, LANES), jnp.float32)
    for b in range(8):
        send_ref[rows(b, 0), :] = dp[b]
        send_ref[rows(b, 1), :] = dq[b]
        prev_ref[0, b] = dp[b]
        prev_ref[1, b] = dq[b]
        m_ref[0, b] = zero
        m_ref[1, b] = zero

    def block(k, carry):
        ps = [prev_ref[0, b] for b in range(8)]
        qs = [prev_ref[1, b] for b in range(8)]
        for _ in range(FACTOR):
            both = [phi_slab(p, q, w0) for p, q in zip(ps, qs)]
            ps, qs = [x[0] for x in both], [x[1] for x in both]
        for b in range(8):
            np_, nq = phi_slab(prev_ref[0, b], prev_ref[1, b], w1)
            mp, mq = phi_slab(m_ref[0, b], m_ref[1, b], w1)
            m_ref[0, b] = mp + (ps[b] - np_)
            m_ref[1, b] = mq + (qs[b] - nq)
            prev_ref[0, b] = np_
            prev_ref[1, b] = nq
        return carry

    lax.fori_loop(0, FACTOR, block, 0)

    rp, rq = [], []
    for b in range(8):
        cp, cq = apply2(send_ref[rows(b, 0), :], send_ref[rows(b, 1), :], w2)
        rp.append(got_ref[rows(b, 2), :] + (m_ref[0, b] + (prev_ref[0, b] - cp)))
        rq.append(got_ref[rows(b, 3), :] + (m_ref[1, b] + (prev_ref[1, b] - cq)))
    dp, dq = recurrence(rp, rq)
    for b in range(8):
        send_ref[rows(b, 2), :] = dp[b]
        send_ref[rows(b, 3), :] = dq[b]


def last_kernel(f_ref, right_ref, left_ref, r1_ref, r2_ref, w_ref, got_ref, out_ref, prev_ref, c_ref, r1b_ref, d_ref):
    lane = lanes_of((TILES, LANES))
    lane1 = lanes_of((1, LANES))
    for c in range(4):
        whole = jnp.zeros((TILES, LANES), jnp.float32)
        for quarter in range(4):
            piece = got_ref[pl.ds(4 * quarter + c, TILES, stride=16), :]
            piece = pltpu.roll(piece, (SLAB * quarter - MARGIN) % LANES, 1)
            mine = (lane >= SLAB * quarter) & (lane < SLAB * (quarter + 1))
            whole = jnp.where(mine, piece, whole)
        d_ref[c, 0:TILES, :] = whole
        d_ref[c, TILES:PACKED, :] = jnp.zeros((PACKED - TILES, LANES), jnp.float32)
        low = pltpu.roll(got_ref[c : c + 1, :], LANES - MARGIN, 1)
        d_ref[c, LEFT : LEFT + 1, :] = jnp.where(lane1 >= LANES - MARGIN, low, 0.0)
        end = (WINDOWS - 1) * 4 + c
        high = pltpu.roll(got_ref[end : end + 1, :], MARGIN, 1)
        d_ref[c, RIGHT : RIGHT + 1, :] = jnp.where(lane1 < MARGIN, high, 0.0)

    weight_of = fine_weights(w_ref)
    w1 = [w_ref[4 + e] for e in range(4)]
    w2 = [w_ref[8 + e] for e in range(4)]
    unused = jnp.zeros(((LEFT - RIGHT - 1) * 8, LANES), jnp.float32)
    for field in range(2):
        r1b_ref[field, (RIGHT + 1) * 8 : LEFT * 8, :] = unused

    p, q = d_ref[0], d_ref[1]
    last_p, last_q = apply2(p, q, w2)
    c_ref[0, pl.ds(FACTOR - 1, PACKED, stride=8), :] = last_p + r2_ref[0]
    c_ref[1, pl.ds(FACTOR - 1, PACKED, stride=8), :] = last_q + r2_ref[1]
    prev_ref[0, pl.ds(0, PACKED, stride=8), :] = p
    prev_ref[1, pl.ds(0, PACKED, stride=8), :] = q
    for k in range(FACTOR - 1):
        p, q = phi_packed(p, q, w1)
        p = p + r1_ref[0, pl.ds(k, PACKED, stride=8), :]
        q = q + r1_ref[1, pl.ds(k, PACKED, stride=8), :]
        c_ref[0, pl.ds(k, PACKED, stride=8), :] = p
        c_ref[1, pl.ds(k, PACKED, stride=8), :] = q
        prev_ref[0, pl.ds(k + 1, PACKED, stride=8), :] = p
        prev_ref[1, pl.ds(k + 1, PACKED, stride=8), :] = q

    ps = [prev_ref[0, tile_rows(t), :] for t in range(LISTED)]
    qs = [prev_ref[1, tile_rows(t), :] for t in range(LISTED)]
    for j in range(FACTOR):
        ps, qs = phi_tiles(ps, qs, weight_of)
        for t in range(LISTED):
            ps[t] = ps[t] + load_forcing(f_ref, right_ref, left_ref, j, t, 0)
            qs[t] = qs[t] + load_forcing(f_ref, right_ref, left_ref, j, t, 1)
            if j < FACTOR - 1 and t < TILES:
                out_ref[pl.ds(j * 32 + t * 2, 8, stride=256), :] = ps[t]
                out_ref[pl.ds(j * 32 + t * 2 + 1, 8, stride=256), :] = qs[t]
    for t in range(LISTED):
        r1b_ref[0, tile_rows(t), :] = ps[t] - c_ref[0, tile_rows(t), :]
        r1b_ref[1, tile_rows(t), :] = qs[t] - c_ref[1, tile_rows(t), :]

    def finish(k, p, q):
        for field, x in enumerate((p, q)):
            done = c_ref[field, pl.ds(k, PACKED, stride=8), :] + x
            out_ref[pl.ds((8 * k + 7) * 32 + field, TILES, stride=2), :] = done[0:TILES]

    p, q = d_ref[2], d_ref[3]
    last_p, last_q = apply2(p, q, w2)
    mp = mq = None
    for k in range(FACTOR):
        rp, rq = r1b_ref[0, pl.ds(k, PACKED, stride=8), :], r1b_ref[1, pl.ds(k, PACKED, stride=8), :]
        if k == 0:
            mp, mq = rp, rq
        else:
            mp, mq = phi_packed(mp, mq, w1)
            mp, mq = mp + rp, mq + rq
        if k < FACTOR - 1:
            p, q = phi_packed(p, q, w1)
            p, q = p + rp, q + rq
            finish(k, p, q)
    finish(FACTOR - 1, last_p + mp, last_q + mq)


VMEM = pl.BlockSpec(memory_space=pltpu.VMEM)
SMEM = pl.BlockSpec(memory_space=pltpu.SMEM)
STATE = (2, PACKED * 8, LANES)


def shaped(*shape):
    return jax.ShapeDtypeStruct(shape, jnp.float32)


def scratch(*shape):
    return pltpu.VMEM(shape, jnp.float32)


def first_stage(flat_blocks, flat, right, left, friction, compressor):
    return pl.pallas_call(
        first_kernel,
        out_shape=(shaped(*STATE), shaped(2, PACKED, LANES), shaped(12, PACKED, LANES), shaped(PACKED, LANES), shaped(4 * WINDOWS, LANES)),
        in_specs=[SMEM] + [VMEM] * 5,
        out_specs=(VMEM,) * 5,
        scratch_shapes=[scratch(*STATE)] * 3,
        name="first",
    )(flat_blocks, flat, right, left, friction, compressor)


def slab_stage(place, flat_blocks, kinds, got):
    return pl.pallas_call(
        slab_kernel,
        out_shape=shaped(4 * WINDOWS, LANES),
        in_specs=[SMEM, SMEM, VMEM, VMEM],
        out_specs=VMEM,
        scratch_shapes=[scratch(2, 8, 8, LANES)] * 2,
        name="slab",
    )(place, flat_blocks, kinds, got)


def last_stage(flat, right, left, r1, r2, weights, got):
    return pl.pallas_call(
        last_kernel,
        out_shape=shaped(2048, LANES),
        in_specs=[VMEM] * 7,
        out_specs=VMEM,
        scratch_shapes=[scratch(*STATE)] * 3 + [scratch(4, PACKED, LANES)],
        name="last",
    )(flat, right, left, r1, r2, weights, got)


def to_rows(forcing):
    return forcing.reshape(64, 2, TILES, LANES).transpose(0, 2, 1, 3).reshape(2048, LANES)


def from_rows(rows):
    return rows.reshape(64, TILES, 2, LANES).transpose(0, 2, 1, 3).reshape(64, 2, TILES * LANES)


def edge_of(flat, kinds, tile):
    sides = flat.reshape(64, 2 * TILES, LANES)[:, 2 * tile : 2 * tile + 2].reshape(128, LANES)
    return jnp.concatenate([sides, jnp.broadcast_to(kinds[tile : tile + 1], (EDGE_ROWS - 128, LANES))])


def one_based(friction, compressor):
    return jnp.where(compressor == 1, KINDS, friction + 1).astype(jnp.float32)


def transpose_windows(rows):
    return lax.all_to_all(rows.reshape(WINDOWS, 4, LANES), "tm", 0, 0).reshape(4 * WINDOWS, LANES)


def per_device(forcing, friction_class, compressor, blocks):
    flat = to_rows(forcing)
    flat_blocks = blocks.reshape(-1)
    friction = friction_class.reshape(TILES, LANES)
    station = compressor.reshape(TILES, LANES)
    kinds = one_based(friction, station)
    count = lax.axis_size("net")
    left = lax.ppermute(edge_of(flat, kinds, TILES - 1), "net", [(i, i + 1) for i in range(count - 1)])
    right = lax.ppermute(edge_of(flat, kinds, 0), "net", [(i + 1, i) for i in range(count - 1)])
    r1, r2, weights, kinds_wide, send = first_stage(flat_blocks, flat, right, left, friction, station)
    got = transpose_windows(send)
    place = lax.axis_index("tm").astype(jnp.int32).reshape(1)
    send = slab_stage(place, flat_blocks, kinds_wide, got)
    got = transpose_windows(send)
    return from_rows(last_stage(flat, right, left, r1, r2, weights, got))


def solution(mesh):
    placed = (P("tm", None, "net"), P("net"), P("net"), P())
    return jax.shard_map(
        per_device, mesh=mesh, in_specs=placed, out_specs=P("tm", None, "net"), check_vma=False
    )
```

profile of v0, /device:TPU:8, one launch (start us, length us, event | category | flops | bytes accessed | tf_op | source)
XLA Modules:
  0.0 84.8 jit_solution(7448112926297401015)
XLA Ops:
  0.0 0.7 select_convert_fusion
  0.7 1.1 %fusion = (f32[64,2,128]{2,1,0:T(2,128)S(1)}, f32[64,2,128]{2,1,0:T(2,128)S(1)}) fusion(f32[64,32,128]{2,1,0:T(8,128)} %bitcast.27), kind=kLoop, calls=%fused_computation.5 | loop fusion | bytes 262144 | tf_op jit(solution)/shard_map/slice | solution.py:398
  1.8 1.9 %collective-permute-start = (f32[136,128]{1,0:T(8,128)S(1)}, f32[136,128]{1,0:T(8,128)S(1)}, u32[]{:S(2)}, u32[]{:S(2)}) collective-permute-start(f32[136,128]{1,0:T(8,128)S(1)} %pad_maximum_fusion), channel_id=1, source_target_pairs={{1,0},{2,1},{3,2},{4,3},{5,4},{6,5},{7,6},{9,8},{10,9},{11,10},{12... | collective-permute-start | bytes 208904 | tf_op jit(solution)/shard_map/ppermute | solution.py:418
  3.8 0.0 copy-start.3
  3.8 2.4 %collective-permute-start.1 = (f32[136,128]{1,0:T(8,128)S(1)}, f32[136,128]{1,0:T(8,128)S(1)}, u32[]{:S(2)}, u32[]{:S(2)}) collective-permute-start(f32[136,128]{1,0:T(8,128)S(1)} %pad_maximum_fusion.1), channel_id=1, source_target_pairs={{0,1},{1,2},{2,3},{3,4},{4,5},{5,6},{6,7},{8,9},{9,10},{10,11},{11... | collective-permute-start | bytes 208904 | tf_op jit(solution)/shard_map/ppermute | solution.py:417
  6.2 0.0 copy-done.3
  6.2 0.6 reshape.48.blocks_ref
  6.8 0.0 collective-permute-done.right_ref
  6.8 0.0 copy-start.1
  6.8 6.8 %collective-permute-done.1.left_ref = f32[136,128]{1,0:T(8,128)S(1)} collective-permute-done((f32[136,128]{1,0:T(8,128)S(1)}, f32[136,128]{1,0:T(8,128)S(1)}, u32[]{:S(2)}, u32[]{:S(2)}) %collective-permute-start.1) | collective-permute-done | bytes 69664 | tf_op jit(solution)/shard_map/ppermute | solution.py:417
  13.6 0.0 copy-start.2
  13.6 0.0 copy-done.1
  13.6 0.6 copy-done.2
  14.2 5.7 %first.1 = (f32[2,192,128]{2,1,0:T(8,128)}, f32[2,24,128]{2,1,0:T(8,128)}, f32[12,24,128]{2,1,0:T(8,128)}, f32[24,128]{1,0:T(8,128)}, f32[256,128]{1,0:T(8,128)}) custom-call(f32[108]{0:T(128)} %reshape.48.blocks_ref, f32[2048,128]{1,0:T(8,128)} %bitcast.28, f32[136,128]{1,0:T(8,128)} %copy-done.1, f32[136,128]{1,0:T(8,128)} %copy-done.2, ...), custom_call_target="tpu_custom_call" | custom-call | tf_op jit(solution)/shard_map/first/pallas_call | solution.py:357
  19.9 14.4 %all-to-all-start = ((f32[64,4,128]{2,1,0:T(4,128)}), f32[64,4,128]{2,1,0:T(4,128)S(1)}, u32[]{:S(2)}, u32[]{:S(2)}) async-start(f32[64,4,128]{2,1,0:T(4,128)} %bitcast.35), calls=%async_computation | async-start | bytes 262144 | tf_op jit(solution)/shard_map/all_to_all | solution.py:407
  34.3 15.9 %all-to-all-done = f32[64,4,128]{2,1,0:T(4,128)S(1)} async-done(((f32[64,4,128]{2,1,0:T(4,128)}), f32[64,4,128]{2,1,0:T(4,128)S(1)}, u32[]{:S(2)}, u32[]{:S(2)}) %all-to-all-start) | async-done | bytes 131104 | tf_op jit(solution)/shard_map/all_to_all | solution.py:407
  50.2 0.0 copy-start
  50.2 0.7 copy-done
  50.9 6.9 %slab.1 = f32[256,128]{1,0:T(8,128)} custom-call(s32[1]{0:T(128)} %bitcast.13.place_ref, f32[108]{0:T(128)} %reshape.48.blocks_ref, f32[24,128]{1,0:T(8,128)} %get-tuple-element.13.kx_ref, f32[256,128]{1,0:T(8,128)} %bitcast.30), custom_call_target="tpu_custom_call" | custom-call | tf_op jit(solution)/shard_map/slab/pallas_call | solution.py:368
  57.8 21.5 %all_to_all.10 = f32[64,4,128]{2,1,0:T(4,128)} all-to-all(f32[64,4,128]{2,1,0:T(4,128)} %bitcast.31), channel_id=1, replica_groups=mesh['tm'=64,'net'=8] {'tm'}, dimensions={0} | all-to-all | bytes 262144 | tf_op jit(solution)/shard_map/all_to_all | solution.py:407
  79.2 5.6 %last.1 = f32[2048,128]{1,0:T(8,128)} custom-call(f32[2048,128]{1,0:T(8,128)} %bitcast.29, f32[136,128]{1,0:T(8,128)} %copy-done.1, f32[136,128]{1,0:T(8,128)} %copy-done.2, f32[2,192,128]{2,1,0:T(8,128)} %get-tuple-element.10.r1_ref, f32[2,24,128]{2,1,0:T(8,128)} %get-tuple-element.11.r2_ref, f32[12,24,128]{2,1,0:T(8,128)} %get-tuple-element.12.w_ref, ...), custom_call_target="tpu_custom_call" | custom-call | tf_op jit(solution)/shard_map/last/pallas_call | solution.py:379
  (5 shorter events, 0.0 us)
Async XLA Ops:
  1.8 5.0 %collective-permute-start = (f32[136,128]{1,0:T(8,128)S(1)}, f32[136,128]{1,0:T(8,128)S(1)}, u32[]{:S(2)}, u32[]{:S(2)}) collective-permute-start(f32[136,128]{1,0:T(8,128)S(1)} %pad_maximum_fusion), channel_id=1, source_target_pairs={{1,0},{2,1},{3,2},{4,3},{5,4},{6,5},{7,6},{9,8},{10,9},{11,10},{12... | collective-permute-start | bytes 208904 | tf_op jit(solution)/shard_map/ppermute | solution.py:418
  3.8 2.4 %copy-start.3 = (f32[3,2,2,9]{3,2,1,0:T(2,128)S(1)}, f32[3,2,2,9]{3,2,1,0:T(2,128)}, u32[]{:S(2)}) copy-start(f32[3,2,2,9]{3,2,1,0:T(2,128)} %param.7) | copy-start | bytes 1300
  3.8 9.8 %collective-permute-start.1 = (f32[136,128]{1,0:T(8,128)S(1)}, f32[136,128]{1,0:T(8,128)S(1)}, u32[]{:S(2)}, u32[]{:S(2)}) collective-permute-start(f32[136,128]{1,0:T(8,128)S(1)} %pad_maximum_fusion.1), channel_id=1, source_target_pairs={{0,1},{1,2},{2,3},{3,4},{4,5},{5,6},{6,7},{8,9},{9,10},{10,11},{11... | collective-permute-start | bytes 208904 | tf_op jit(solution)/shard_map/ppermute | solution.py:417
  6.8 6.8 %copy-start.1 = (f32[136,128]{1,0:T(8,128)}, f32[136,128]{1,0:T(8,128)S(1)}, u32[]{:S(2)}) copy-start(f32[136,128]{1,0:T(8,128)S(1)} %collective-permute-done.right_ref) | copy-start | bytes 208900
  13.6 0.6 copy-start.2
  19.9 30.3 %all-to-all-start = ((f32[64,4,128]{2,1,0:T(4,128)}), f32[64,4,128]{2,1,0:T(4,128)S(1)}, u32[]{:S(2)}, u32[]{:S(2)}) async-start(f32[64,4,128]{2,1,0:T(4,128)} %bitcast.35), calls=%async_computation | async-start | bytes 262144 | tf_op jit(solution)/shard_map/all_to_all | solution.py:407
  50.2 0.7 copy-start
where the time goes:
time: 85.2 us; the launch traced here: 84.8 us
  waiting for transfers between devices  22.7 us (27%)
  blocking collectives  21.5 us (25%)
  starting transfers between devices  18.7 us (22%)
  Pallas kernels  18.1 us (21%)
  local copies, waits for them, and re-layouts  2.97 us (3%)
    all_to_all x1, blocking collectives, transpose_windows(): lax.all_to_all(rows.reshape(WINDOWS, 4, LANES), 'tm', 0, 0)  21.5 us
    all_to_all x1, waiting for transfers between devices, transpose_windows(): lax.all_to_all(rows.reshape(WINDOWS, 4, LANES), 'tm', 0, 0)  15.9 us
    all_to_all x1, starting transfers between devices, transpose_windows(): lax.all_to_all(rows.reshape(WINDOWS, 4, LANES), 'tm', 0, 0)  14.4 us
    pallas_call x1, Pallas kernels, slab_stage(): pl.pallas_call(slab_kernel, out_shape=shaped(4 * WINDOWS, LANES), in_spec...  6.88 us
    ppermute x1, waiting for transfers between devices, per_device(): lax.ppermute(edge_of(flat, kinds, TILES - 1), 'net', [(i, i + 1) for i in...  6.77 us
    pallas_call x1, Pallas kernels, first_stage(): pl.pallas_call(first_kernel, out_shape=(shaped(*STATE), shaped(2, PACKED,...  5.67 us
    pallas_call x1, Pallas kernels, last_stage(): pl.pallas_call(last_kernel, out_shape=shaped(2048, LANES), in_specs=[VMEM...  5.59 us
    ppermute x1, starting transfers between devices, per_device(): lax.ppermute(edge_of(flat, kinds, TILES - 1), 'net', [(i, i + 1) for i in...  2.41 us
  transfers between devices with their start and end apart: 3, of which 2 were waited for; matrix products, arithmetic and copies ran while one was open for 1% of the time, Pallas kernels for 0%

commit v1 on v0

v1 whole, which is shorter than its diff:
```python
import jax
import jax.numpy as jnp
from jax import lax
from jax.experimental import pallas as pl
from jax.experimental.pallas import tpu as pltpu
from jax.sharding import PartitionSpec as P

FACTOR = 8
KINDS = 9
LANES = 128
TILES = 16
WINDOWS = 64
PACKED = 24
RIGHT = 16
LEFT = 23
EDGE_ROWS = 136
STRIDE = 264
PADDED = FACTOR * STRIDE
ROWS_OF = list(range(TILES)) + [RIGHT, LEFT]
LISTED = len(ROWS_OF)
PREV = [LISTED - 1] + list(range(TILES)) + [LISTED - 1]
NEXT = list(range(1, TILES + 1)) + [TILES, 0]
SLAB = 32
REACH = 22
SPAN = 84
COMB = 48
GROUPS = 2 * COMB // 8
PAIR = 2


def lanes_of(shape):
    return lax.broadcasted_iota(jnp.int32, shape, len(shape) - 1)


def couple(p, q, p_low, p_high, q_low, q_high, w):
    mixed_p = (p + p) + (q_high - q_low)
    mixed_q = (q + q) + (p_low - p_high)
    return w[0] * mixed_p + w[1] * mixed_q, w[2] * mixed_p + w[3] * mixed_q


def apply2(p, q, w):
    return w[0] * p + w[1] * q, w[2] * p + w[3] * q


def phi_tiles(ps, qs, weight_of):
    lane = lanes_of((8, LANES))
    first, last = lane == 0, lane == LANES - 1

    def low(xs, t):
        return pltpu.roll(jnp.where(last, xs[PREV[t]], xs[t]), 1, 1)

    def high(xs, t):
        return pltpu.roll(jnp.where(first, xs[NEXT[t]], xs[t]), LANES - 1, 1)

    new_p, new_q = [], []
    for t in range(LISTED):
        p, q = couple(ps[t], qs[t], low(ps, t), high(ps, t), low(qs, t), high(qs, t), weight_of(t))
        new_p.append(p)
        new_q.append(q)
    return new_p, new_q


def phi_packed(p, q, w):
    lane = lanes_of((PACKED, LANES))
    first, last = lane == 0, lane == LANES - 1

    def low(x):
        return pltpu.roll(jnp.where(last, pltpu.roll(x, 1, 0), x), 1, 1)

    def high(x):
        return pltpu.roll(jnp.where(first, pltpu.roll(x, PACKED - 1, 0), x), LANES - 1, 1)

    return couple(p, q, low(p), high(p), low(q), high(q), w)


def phi_slab(p, q, w):
    return couple(
        p, q, pltpu.roll(p, 1, 1), pltpu.roll(p, LANES - 1, 1), pltpu.roll(q, 1, 1), pltpu.roll(q, LANES - 1, 1), w
    )


def pick(blocks_ref, number, kind):
    scale = 1.0 if number == 2 else 0.25
    masks = [kind == float(k + 1) for k in range(KINDS)]
    picked = []
    for entry in range(4):
        chosen = jnp.zeros_like(kind)
        for k in range(KINDS):
            chosen = jnp.where(masks[k], blocks_ref[(number * 4 + entry) * KINDS + k] * scale, chosen)
        picked.append(chosen)
    return picked


def load_forcing(f_ref, right_ref, left_ref, j, t, field):
    if t < TILES:
        return f_ref[pl.ds(j * 32 + t * 2 + field, 8, stride=STRIDE), :]
    edge = right_ref if t == TILES else left_ref
    return edge[pl.ds((j * 2 + field) * 8, 8), :]


def tile_rows(t):
    return pl.ds(ROWS_OF[t] * 8, 8)


def fine_weights(w_ref):
    def weight_of(t):
        return [jnp.broadcast_to(w_ref[e, ROWS_OF[t] : ROWS_OF[t] + 1, :], (8, LANES)) for e in range(4)]

    return weight_of


def edge_kernel(source_ref, fc_hbm, comp_hbm, f_ref, low_ref, high_ref, kind_ref, fc_ref, comp_ref, sems):
    copies = [
        pltpu.make_async_copy(source_ref.at[pl.ds(k * 256, 256)], f_ref.at[pl.ds(k * STRIDE, 256)], sems.at[k])
        for k in range(FACTOR)
    ]
    labels = [
        pltpu.make_async_copy(fc_hbm, fc_ref, sems.at[FACTOR]),
        pltpu.make_async_copy(comp_hbm, comp_ref, sems.at[FACTOR + 1]),
    ]
    for copy in labels + copies:
        copy.start()
    for copy in labels:
        copy.wait()
    kinds = jnp.where(comp_ref[...] == 1, KINDS, fc_ref[...] + 1).astype(jnp.float32)
    kind_ref[...] = kinds
    low_ref[128:EDGE_ROWS, :] = jnp.broadcast_to(kinds[0:1], (8, LANES))
    high_ref[128:EDGE_ROWS, :] = jnp.broadcast_to(kinds[TILES - 1 : TILES], (8, LANES))
    for copy in copies:
        copy.wait()
    for j in range(FACTOR):
        for field in range(2):
            rows = pl.ds((j * 2 + field) * 8, 8)
            low_ref[rows, :] = f_ref[pl.ds(j * 32 + field, 8, stride=STRIDE), :]
            high_ref[rows, :] = f_ref[pl.ds(j * 32 + 2 * (TILES - 1) + field, 8, stride=STRIDE), :]


def first_kernel(blocks_ref, f_ref, right_ref, left_ref, kind_ref, r1_ref, r2_ref, w_ref, kx_ref, send_ref,
                 prev_ref, c_ref, r1b_ref):
    kx_ref[0:TILES, :] = kind_ref[...]
    kx_ref[TILES:PACKED, :] = jnp.zeros((PACKED - TILES, LANES), jnp.float32)
    kx_ref[RIGHT : RIGHT + 1, :] = right_ref[128:129, :]
    kx_ref[LEFT : LEFT + 1, :] = left_ref[128:129, :]
    kind = kx_ref[...]
    for number in range(3):
        for entry, chosen in enumerate(pick(blocks_ref, number, kind)):
            w_ref[number * 4 + entry] = chosen
    weight_of = fine_weights(w_ref)
    w1 = [w_ref[4 + e] for e in range(4)]

    def forcing(j, field):
        return [load_forcing(f_ref, right_ref, left_ref, j, t, field) for t in range(LISTED)]

    unused = jnp.zeros(((LEFT - RIGHT - 1) * 8, LANES), jnp.float32)
    for field in range(2):
        for ref in (r1_ref, r1b_ref):
            ref[field, (RIGHT + 1) * 8 : LEFT * 8, :] = unused

    ps, qs = forcing(0, 0), forcing(0, 1)
    for j in range(1, FACTOR):
        ps, qs = phi_tiles(ps, qs, weight_of)
        fp, fq = forcing(j, 0), forcing(j, 1)
        ps = [a + b for a, b in zip(ps, fp)]
        qs = [a + b for a, b in zip(qs, fq)]
    for t in range(LISTED):
        r1_ref[0, tile_rows(t), :] = ps[t]
        r1_ref[1, tile_rows(t), :] = qs[t]

    def sweep(ref, keep):
        p = q = None
        for k in range(FACTOR):
            rp, rq = ref[0, pl.ds(k, PACKED, stride=8), :], ref[1, pl.ds(k, PACKED, stride=8), :]
            if k == 0:
                p, q = rp, rq
            else:
                p, q = phi_packed(p, q, w1)
                p, q = p + rp, q + rq
            if keep:
                c_ref[0, pl.ds(k, PACKED, stride=8), :] = p
                c_ref[1, pl.ds(k, PACKED, stride=8), :] = q
                if k < FACTOR - 1:
                    prev_ref[0, pl.ds(k + 1, PACKED, stride=8), :] = p
                    prev_ref[1, pl.ds(k + 1, PACKED, stride=8), :] = q
        return p, q

    nothing = jnp.zeros((PACKED, LANES), jnp.float32)
    prev_ref[0, pl.ds(0, PACKED, stride=8), :] = nothing
    prev_ref[1, pl.ds(0, PACKED, stride=8), :] = nothing
    r2p, r2q = sweep(r1_ref, True)
    r2_ref[0] = r2p
    r2_ref[1] = r2q

    ps = [prev_ref[0, tile_rows(t), :] for t in range(LISTED)]
    qs = [prev_ref[1, tile_rows(t), :] for t in range(LISTED)]
    for j in range(FACTOR):
        ps, qs = phi_tiles(ps, qs, weight_of)
    for field, xs in enumerate((ps, qs)):
        for t in range(LISTED):
            rows = tile_rows(t)
            r1b_ref[field, rows, :] = xs[t] + (r1_ref[field, rows, :] - c_ref[field, rows, :])
    gp, gq = sweep(r1b_ref, False)

    lane = lanes_of((8, LANES))
    for c, (x, g) in enumerate(((r2p, gp), (r2q, gq))):
        for half in range(2):
            shifted = [
                [y[8 * half : 8 * half + 8] for y in (pltpu.roll(z, 1, 0), z, pltpu.roll(z, PACKED - 1, 0))]
                for z in (x, g)
            ]

            def window(which, offset):
                a, b = shifted[which][0:2] if offset < 0 else shifted[which][1:3]
                start = offset % LANES
                return pltpu.roll(jnp.where(lane >= start, a, b), (LANES - start) % LANES, 1)

            for quarter in range(4):
                origin = SLAB * quarter
                near = window(0, origin + window_start(half))
                far = window(1, origin + share_start(half) - SPAN)
                send_ref[pl.ds(64 * half + 2 * quarter + c, 8, stride=8), :] = jnp.where(lane < SPAN, near, far)


def window_start(half):
    return -REACH if half else -REACH - 8


def share_start(half):
    return 0 if half else -8


def prepare_kernel(place_ref, blocks_ref, kx_ref, scan_ref, dense_ref, prev_ref, m_ref):
    place = place_ref[0]
    lane1 = lanes_of((1, LANES))
    origin = place * SLAB + (LANES - REACH - 8) + jnp.where(place >= WINDOWS // 2, 8, 0)
    base = origin // LANES - 1
    start = origin % LANES
    base = jnp.where(base < 0, LEFT, base)
    after = jnp.where(base == LEFT, 0, base + 1)
    a, b = kx_ref[pl.ds(base, 1), :], kx_ref[pl.ds(after, 1), :]
    kind = pltpu.roll(jnp.where(lane1 >= start, a, b), LANES - start, 1)
    kind = jnp.broadcast_to(kind, (8, LANES))
    w0, w1, w2 = (pick(blocks_ref, number, kind) for number in range(3))
    sub = lax.broadcasted_iota(jnp.int32, (8, LANES), 0)
    lane = lanes_of((8, LANES))

    def times(v, w):
        return [
            v[0] * w[0] + v[1] * w[2],
            v[0] * w[1] + v[1] * w[3],
            v[2] * w[0] + v[3] * w[2],
            v[2] * w[1] + v[3] * w[3],
        ]

    one, none = jnp.ones((8, LANES), jnp.float32), jnp.zeros((8, LANES), jnp.float32)
    w = w2
    grown = [one, none, none, one]
    for n, step in enumerate((1, 2, 4)):
        longer = times(grown, w)
        grown = [jnp.where((sub & step) != 0, x, y) for x, y in zip(longer, grown)]
        for e in range(4):
            scan_ref[4 * n + e] = jnp.where(sub >= step, w[e], 0.0)
        w = times(w, w)
    for e in range(4):
        scan_ref[12 + e] = w[e]
        scan_ref[16 + e] = grown[e]

    combs = []
    for n in range(COMB // 8):
        at = sub + 8 * n
        combs.append(jnp.where((lane == at) | (lane == at + COMB), 1.0, 0.0))
    start_p = combs + [none] * (COMB // 8)
    start_q = [none] * (COMB // 8) + combs
    for n in range(GROUPS):
        prev_ref[0, n] = start_p[n]
        prev_ref[1, n] = start_q[n]
        m_ref[0, n] = none
        m_ref[1, n] = none

    def block(k, carry):
        ps, qs, after_p, after_q = [], [], [], []
        for n in range(GROUPS):
            p, q = prev_ref[0, n], prev_ref[1, n]
            for _ in range(PAIR):
                ps.append(p)
                qs.append(q)
                p, q = phi_slab(p, q, w1)
                after_p.append(p)
                after_q.append(q)
            prev_ref[0, n] = p
            prev_ref[1, n] = q
        for _ in range(FACTOR):
            both = [phi_slab(p, q, w0) for p, q in zip(ps, qs)]
            ps, qs = [x[0] for x in both], [x[1] for x in both]
        for n in range(GROUPS):
            p, q = m_ref[0, n], m_ref[1, n]
            for e in range(PAIR * n, PAIR * n + PAIR):
                p, q = phi_slab(p, q, w1)
                p, q = p + (ps[e] - after_p[e]), q + (qs[e] - after_q[e])
            m_ref[0, n] = p
            m_ref[1, n] = q
        return carry

    lax.fori_loop(0, FACTOR // PAIR, block, 0)

    for n in range(GROUPS):
        field, c = divmod(n, COMB // 8)
        cp, cq = apply2(start_p[n], start_q[n], w2)
        answers = m_ref[0, n] + (prev_ref[0, n] - cp), m_ref[1, n] + (prev_ref[1, n] - cq)
        for tooth in range(2):
            at = sub + (8 * c + COMB * tooth)
            near = (lane - at <= REACH) & (at - lane <= REACH)
            rows = pl.ds(field * LANES + COMB * tooth + 8 * c, 8)
            for to in range(2):
                dense_ref[rows, LANES * to : LANES * (to + 1)] = jnp.where(near, answers[to], 0.0)
    for field in range(2):
        dense_ref[field * LANES + 2 * COMB : (field + 1) * LANES, :] = jnp.zeros((LANES - 2 * COMB, 2 * LANES), jnp.float32)


def slab_kernel(scan_ref, dense_ref, got_ref, send_ref, d_ref):
    lane = lanes_of((8, LANES))
    masked = [[scan_ref[4 * n + e] for e in range(4)] for n in range(3)]
    w_eight = [scan_ref[12 + e] for e in range(4)]
    grown = [scan_ref[16 + e] for e in range(4)]
    first = lax.broadcasted_iota(jnp.int32, (8, LANES), 0) == 0

    def recurrence(rp, rq):
        yp, yq = list(rp), list(rq)
        for n, step in enumerate((1, 2, 4)):
            for b in range(8):
                sp, sq = apply2(pltpu.roll(yp[b], step, 0), pltpu.roll(yq[b], step, 0), masked[n])
                yp[b], yq[b] = yp[b] + sp, yq[b] + sq
        dp, dq = [], []
        tp = tq = None
        for b in range(8):
            bp, bq = pltpu.roll(yp[b], 1, 0), pltpu.roll(yq[b], 1, 0)
            bp, bq = jnp.where(first, 0.0, bp), jnp.where(first, 0.0, bq)
            ep, eq = yp[b][7:8], yq[b][7:8]
            ep, eq = jnp.broadcast_to(ep, (8, LANES)), jnp.broadcast_to(eq, (8, LANES))
            if b:
                sp, sq = apply2(tp, tq, grown)
                bp, bq = bp + sp, bq + sq
                sp, sq = apply2(tp, tq, w_eight)
                ep, eq = ep + sp, eq + sq
            tp, tq = ep, eq
            dp.append(bp)
            dq.append(bq)
        return dp, dq

    def rows(b, c):
        return pl.ds(b * 16 + c, 8, stride=2)

    gotten = [[got_ref[rows(b, c), :] for b in range(8)] for c in range(2)]
    dp, dq = recurrence(*gotten)
    for b in range(8):
        d_ref[8 * b : 8 * b + 8, 0:LANES] = dp[b]
        d_ref[8 * b : 8 * b + 8, LANES : 2 * LANES] = dq[b]
    answer = jnp.dot(d_ref[...], dense_ref[...], precision=lax.Precision.HIGHEST, preferred_element_type=jnp.float32)
    back = SPAN - REACH
    residual = [
        [
            answer[8 * b : 8 * b + 8, LANES * c : LANES * (c + 1)] + pltpu.roll(gotten[c][b], LANES - back, 1)
            for b in range(8)
        ]
        for c in range(2)
    ]
    ep, eq = recurrence(*residual)
    for b in range(8):
        send_ref[rows(b, 0), :] = jnp.where(lane < SPAN, dp[b], pltpu.roll(ep[b], back, 1))
        send_ref[rows(b, 1), :] = jnp.where(lane < SPAN, dq[b], pltpu.roll(eq[b], back, 1))


def last_kernel(f_ref, right_ref, left_ref, r1_ref, r2_ref, w_ref, got_ref, out_ref, prev_ref, c_ref, r1b_ref, d_ref,
                o_ref, sems):
    lane = lanes_of((8, LANES))
    lane1 = lanes_of((1, LANES))
    for c in range(2):
        for cycle in range(2):
            for half in range(2):
                begin = (SPAN - share_start(half)) if cycle else -window_start(half)
                whole = jnp.zeros((8, LANES), jnp.float32)
                for quarter in range(4):
                    piece = got_ref[pl.ds(64 * half + 2 * quarter + c, 8, stride=8), :]
                    piece = pltpu.roll(piece, (SLAB * quarter - begin) % LANES, 1)
                    mine = (lane >= SLAB * quarter) & (lane < SLAB * (quarter + 1))
                    whole = jnp.where(mine, piece, whole)
                d_ref[2 * cycle + c, 8 * half : 8 * half + 8, :] = whole
            d_ref[2 * cycle + c, TILES:PACKED, :] = jnp.zeros((PACKED - TILES, LANES), jnp.float32)
            width = 8 if cycle else 24
            begin = (SPAN - share_start(0)) if cycle else -window_start(0)
            low = pltpu.roll(got_ref[c : c + 1, :], LANES - begin, 1)
            d_ref[2 * cycle + c, LEFT : LEFT + 1, :] = jnp.where(lane1 >= LANES - width, low, 0.0)
            begin = (SPAN - share_start(1)) if cycle else -window_start(1)
            end = (WINDOWS - 1) * 2 + c
            high = pltpu.roll(got_ref[end : end + 1, :], LANES - begin - SLAB, 1)
            d_ref[2 * cycle + c, RIGHT : RIGHT + 1, :] = jnp.where(lane1 < width, high, 0.0)

    weight_of = fine_weights(w_ref)
    w1 = [w_ref[4 + e] for e in range(4)]
    w2 = [w_ref[8 + e] for e in range(4)]
    unused = jnp.zeros(((LEFT - RIGHT - 1) * 8, LANES), jnp.float32)
    for field in range(2):
        r1b_ref[field, (RIGHT + 1) * 8 : LEFT * 8, :] = unused

    p, q = d_ref[0], d_ref[1]
    last_p, last_q = apply2(p, q, w2)
    c_ref[0, pl.ds(FACTOR - 1, PACKED, stride=8), :] = last_p + r2_ref[0]
    c_ref[1, pl.ds(FACTOR - 1, PACKED, stride=8), :] = last_q + r2_ref[1]
    prev_ref[0, pl.ds(0, PACKED, stride=8), :] = p
    prev_ref[1, pl.ds(0, PACKED, stride=8), :] = q
    for k in range(FACTOR - 1):
        p, q = phi_packed(p, q, w1)
        p = p + r1_ref[0, pl.ds(k, PACKED, stride=8), :]
        q = q + r1_ref[1, pl.ds(k, PACKED, stride=8), :]
        c_ref[0, pl.ds(k, PACKED, stride=8), :] = p
        c_ref[1, pl.ds(k, PACKED, stride=8), :] = q
        prev_ref[0, pl.ds(k + 1, PACKED, stride=8), :] = p
        prev_ref[1, pl.ds(k + 1, PACKED, stride=8), :] = q

    ps = [prev_ref[0, tile_rows(t), :] for t in range(LISTED)]
    qs = [prev_ref[1, tile_rows(t), :] for t in range(LISTED)]
    for j in range(FACTOR):
        ps, qs = phi_tiles(ps, qs, weight_of)
        if j == FACTOR - 1:
            copies = [
                pltpu.make_async_copy(o_ref.at[pl.ds(k * STRIDE, 224)], out_ref.at[pl.ds(k * 256, 224)], sems.at[k])
                for k in range(FACTOR)
            ]
            for copy in copies:
                copy.start()
        for t in range(LISTED):
            ps[t] = ps[t] + load_forcing(f_ref, right_ref, left_ref, j, t, 0)
            qs[t] = qs[t] + load_forcing(f_ref, right_ref, left_ref, j, t, 1)
            if j < FACTOR - 1 and t < TILES:
                o_ref[pl.ds(j * 32 + t * 2, 8, stride=STRIDE), :] = ps[t]
                o_ref[pl.ds(j * 32 + t * 2 + 1, 8, stride=STRIDE), :] = qs[t]
    for t in range(LISTED):
        r1b_ref[0, tile_rows(t), :] = ps[t] - c_ref[0, tile_rows(t), :]
        r1b_ref[1, tile_rows(t), :] = qs[t] - c_ref[1, tile_rows(t), :]

    def finish(k, p, q):
        for field, x in enumerate((p, q)):
            done = c_ref[field, pl.ds(k, PACKED, stride=8), :] + x
            o_ref[pl.ds(k * STRIDE + 224 + field, TILES, stride=2), :] = done[0:TILES]
        copy = pltpu.make_async_copy(
            o_ref.at[pl.ds(k * STRIDE + 224, 32)], out_ref.at[pl.ds(k * 256 + 224, 32)], sems.at[FACTOR + k]
        )
        copy.start()
        copies.append(copy)

    p, q = d_ref[2], d_ref[3]
    last_p, last_q = apply2(p, q, w2)
    mp = mq = None
    for k in range(FACTOR):
        rp, rq = r1b_ref[0, pl.ds(k, PACKED, stride=8), :], r1b_ref[1, pl.ds(k, PACKED, stride=8), :]
        if k == 0:
            mp, mq = rp, rq
        else:
            mp, mq = phi_packed(mp, mq, w1)
            mp, mq = mp + rp, mq + rq
        if k < FACTOR - 1:
            p, q = phi_packed(p, q, w1)
            p, q = p + rp, q + rq
            finish(k, p, q)
    finish(FACTOR - 1, last_p + mp, last_q + mq)
    for copy in copies:
        copy.wait()


VMEM = pl.BlockSpec(memory_space=pltpu.VMEM)
SMEM = pl.BlockSpec(memory_space=pltpu.SMEM)
STATE = (2, PACKED * 8, LANES)


def shaped(*shape):
    return jax.ShapeDtypeStruct(shape, jnp.float32)


def scratch(*shape):
    return pltpu.VMEM(shape, jnp.float32)


ANY = pl.BlockSpec(memory_space=pl.ANY)
HBM = pl.BlockSpec(memory_space=pltpu.HBM)
SMALL = pltpu.CompilerParams(vmem_limit_bytes=8 << 20)


def edge_stage(flat, friction, compressor):
    return pl.pallas_call(
        edge_kernel,
        out_shape=(shaped(PADDED, LANES), shaped(EDGE_ROWS, LANES), shaped(EDGE_ROWS, LANES), shaped(TILES, LANES)),
        in_specs=[HBM] * 3,
        out_specs=(VMEM,) * 4,
        scratch_shapes=[pltpu.VMEM((TILES, LANES), jnp.int32)] * 2 + [pltpu.SemaphoreType.DMA((FACTOR + 2,))],
        compiler_params=SMALL,
        name="edge",
    )(flat, friction, compressor)


def first_stage(flat_blocks, padded, right, left, kinds):
    return pl.pallas_call(
        first_kernel,
        out_shape=(shaped(*STATE), shaped(2, PACKED, LANES), shaped(12, PACKED, LANES), shaped(PACKED, LANES), shaped(2 * WINDOWS, LANES)),
        in_specs=[SMEM] + [VMEM] * 4,
        out_specs=(VMEM,) * 5,
        scratch_shapes=[scratch(*STATE)] * 3,
        compiler_params=SMALL,
        name="first",
    )(flat_blocks, padded, right, left, kinds)


def prepare_stage(place, flat_blocks, kinds):
    return pl.pallas_call(
        prepare_kernel,
        out_shape=(shaped(20, 8, LANES), shaped(2 * LANES, 2 * LANES)),
        in_specs=[SMEM, SMEM, VMEM],
        out_specs=(VMEM, VMEM),
        scratch_shapes=[scratch(2, GROUPS, 8, LANES)] * 2,
        compiler_params=SMALL,
        name="prepare",
    )(place, flat_blocks, kinds)


def slab_stage(scan, dense, got):
    return pl.pallas_call(
        slab_kernel,
        out_shape=shaped(2 * WINDOWS, LANES),
        in_specs=[VMEM] * 3,
        out_specs=VMEM,
        scratch_shapes=[scratch(WINDOWS, 2 * LANES)],
        compiler_params=SMALL,
        name="slab",
    )(scan, dense, got)


def last_stage(padded, right, left, r1, r2, weights, got):
    return pl.pallas_call(
        last_kernel,
        out_shape=shaped(2048, LANES),
        in_specs=[VMEM] * 7,
        out_specs=ANY,
        scratch_shapes=[scratch(*STATE)] * 3
        + [scratch(4, PACKED, LANES), scratch(PADDED, LANES), pltpu.SemaphoreType.DMA((2 * FACTOR,))],
        compiler_params=SMALL,
        name="last",
    )(padded, right, left, r1, r2, weights, got)


def to_rows(forcing):
    return forcing.reshape(64, 2, TILES, LANES).transpose(0, 2, 1, 3).reshape(2048, LANES)


def from_rows(rows):
    return rows.reshape(64, TILES, 2, LANES).transpose(0, 2, 1, 3).reshape(64, 2, TILES * LANES)


def transpose_windows(rows):
    return lax.all_to_all(rows.reshape(WINDOWS, 2, LANES), "tm", 0, 0).reshape(2 * WINDOWS, LANES)


def per_device(forcing, friction_class, compressor, blocks):
    flat = to_rows(forcing)
    flat_blocks = blocks.reshape(-1)
    friction = friction_class.reshape(TILES, LANES)
    station = compressor.reshape(TILES, LANES)
    count = lax.axis_size("net")
    flat, friction, station = (pltpu.with_memory_space_constraint(x, pltpu.HBM) for x in (flat, friction, station))
    padded, low, high, kinds = edge_stage(flat, friction, station)
    left = lax.ppermute(high, "net", [(i, i + 1) for i in range(count - 1)])
    right = lax.ppermute(low, "net", [(i + 1, i) for i in range(count - 1)])
    r1, r2, weights, kinds_wide, send = first_stage(flat_blocks, padded, right, left, kinds)
    got = transpose_windows(send)
    place = lax.axis_index("tm").astype(jnp.int32).reshape(1)
    scan, dense = prepare_stage(place, flat_blocks, kinds_wide)
    got = transpose_windows(slab_stage(scan, dense, got))
    return from_rows(last_stage(padded, right, left, r1, r2, weights, got))


def solution(mesh):
    placed = (P("tm", None, "net"), P("net"), P("net"), P())
    return jax.shard_map(
        per_device, mesh=mesh, in_specs=placed, out_specs=P("tm", None, "net"), check_vma=False
    )
```

time: 85.2 us -> 72.7 us (0.85)
  the two profiles are of different devices: /device:TPU:8 before, /device:TPU:24 now
where the time goes in v1:
time: 72.7 us; the launch traced here: 72.3 us
  starting transfers between devices  22.9 us (31%)
  blocking collectives  21.6 us (30%)
  Pallas kernels  16.4 us (23%)
  waiting for transfers between devices  10.7 us (15%)
  local copies, waits for them, and re-layouts  0.78 us (1%)
    all_to_all x1, blocking collectives, transpose_windows(): lax.all_to_all(rows.reshape(WINDOWS, 2, LANES), 'tm', 0, 0)  21.6 us
    all_to_all x1, starting transfers between devices, transpose_windows(): lax.all_to_all(rows.reshape(WINDOWS, 2, LANES), 'tm', 0, 0)  18.6 us
    all_to_all x1, waiting for transfers between devices, transpose_windows(): lax.all_to_all(rows.reshape(WINDOWS, 2, LANES), 'tm', 0, 0)  8.07 us
    pallas_call x1, Pallas kernels, prepare_stage(): pl.pallas_call(prepare_kernel, out_shape=(shaped(20, 8, LANES), shaped(2...  6.59 us
    pallas_call x1, Pallas kernels, first_stage(): pl.pallas_call(first_kernel, out_shape=(shaped(*STATE), shaped(2, PACKED,...  4.68 us
    pallas_call x1, Pallas kernels, last_stage(): pl.pallas_call(last_kernel, out_shape=shaped(2048, LANES), in_specs=[VMEM...  3.28 us
    ppermute x1, waiting for transfers between devices, per_device(): left = lax.ppermute(high, 'net', [(i, i + 1) for i in range(count - 1)])  2.59 us
    ppermute x1, starting transfers between devices, per_device(): left = lax.ppermute(high, 'net', [(i, i + 1) for i in range(count - 1)])  2.24 us
  transfers between devices with their start and end apart: 3, of which 2 were waited for; matrix products, arithmetic and copies ran while one was open for 1% of the time, Pallas kernels for 9%

profile of v1, /device:TPU:24, one launch (start us, length us, event | category | flops | bytes accessed | tf_op | source)
XLA Modules:
  0.0 72.3 jit_solution(16827951651857897960)
XLA Ops:
  0.0 1.4 %edge.1 = (f32[2112,128]{1,0:T(8,128)S(1)}, f32[136,128]{1,0:T(8,128)S(1)}, f32[136,128]{1,0:T(8,128)S(1)}, f32[16,128]{1,0:T(8,128)S(1)}) custom-call(f32[2048,128]{1,0:T(8,128)} %bitcast.20, s32[16,128]{1,0:T(8,128)} %bitcast.21, s32[16,128]{1,0:T(8,128)} %bitcast.22), custom_call_target="tpu_custom_call" | custom-call | tf_op jit(solution)/shard_map/edge/pallas_call | solution.py:488
  1.4 2.1 %collective-permute-start = (f32[136,128]{1,0:T(8,128)S(1)}, f32[136,128]{1,0:T(8,128)S(1)}, u32[]{:S(2)}, u32[]{:S(2)}) collective-permute-start(f32[136,128]{1,0:T(8,128)S(1)} %get-tuple-element.17), channel_id=1, source_target_pairs={{1,0},{2,1},{3,2},{4,3},{5,4},{6,5},{7,6},{9,8},{10,9},{11,10},{12... | collective-permute-start | bytes 208904 | tf_op jit(solution)/shard_map/ppermute | solution.py:569
  3.5 2.2 %collective-permute-start.1 = (f32[136,128]{1,0:T(8,128)S(1)}, f32[136,128]{1,0:T(8,128)S(1)}, u32[]{:S(2)}, u32[]{:S(2)}) collective-permute-start(f32[136,128]{1,0:T(8,128)S(1)} %get-tuple-element.18), channel_id=1, source_target_pairs={{0,1},{1,2},{2,3},{3,4},{4,5},{5,6},{6,7},{8,9},{9,10},{10,11},{11... | collective-permute-start | bytes 208904 | tf_op jit(solution)/shard_map/ppermute | solution.py:568
  5.8 0.8 %reshape.40.blocks_ref = f32[108]{0:T(128)S(1)} reshape(f32[3,2,2,9]{3,2,1,0:T(2,128)} %param.7) | data formatting | bytes 864 | tf_op jit(solution)/shard_map/reshape | solution.py:562
  6.5 0.0 collective-permute-done.right_ref
  6.6 2.6 %collective-permute-done.1.left_ref = f32[136,128]{1,0:T(8,128)S(1)} collective-permute-done((f32[136,128]{1,0:T(8,128)S(1)}, f32[136,128]{1,0:T(8,128)S(1)}, u32[]{:S(2)}, u32[]{:S(2)}) %collective-permute-start.1) | collective-permute-done | bytes 69664 | tf_op jit(solution)/shard_map/ppermute | solution.py:568
  9.2 4.7 %first.1 = (f32[2,192,128]{2,1,0:T(8,128)S(1)}, f32[2,24,128]{2,1,0:T(8,128)S(1)}, f32[12,24,128]{2,1,0:T(8,128)S(1)}, f32[24,128]{1,0:T(8,128)S(1)}, f32[128,128]{1,0:T(8,128)}) custom-call(f32[108]{0:T(128)S(1)} %reshape.40.blocks_ref, f32[2112,128]{1,0:T(8,128)S(1)} %get-tuple-element.16.f_ref, f32[136,128]{1,0:T(8,128)S(1)} %collective-permute-done.right_ref, ...), custom_call_target="tpu_custom_call" | custom-call | tf_op jit(solution)/shard_map/first/pallas_call | solution.py:500
  13.8 18.6 %all-to-all-start = ((f32[64,2,128]{2,1,0:T(2,128)}), f32[64,2,128]{2,1,0:T(2,128)S(1)}, u32[]{:S(2)}, u32[]{:S(2)}) async-start(f32[64,2,128]{2,1,0:T(2,128)} %bitcast.6), calls=%async_computation | async-start | bytes 131072 | tf_op jit(solution)/shard_map/all_to_all | solution.py:557
  32.4 6.6 %prepare.1 = (f32[20,8,128]{2,1,0:T(8,128)S(1)}, f32[256,256]{1,0:T(8,128)S(1)}) custom-call(s32[1]{0:T(128)} %bitcast.5.place_ref, f32[108]{0:T(128)S(1)} %reshape.40.blocks_ref, f32[24,128]{1,0:T(8,128)S(1)} %get-tuple-element.23.kx_ref), custom_call_target="tpu_custom_call" | custom-call | tf_op jit(solution)/shard_map/prepare/pallas_call | solution.py:512
  39.0 8.1 %all-to-all-done = f32[64,2,128]{2,1,0:T(2,128)S(1)} async-done(((f32[64,2,128]{2,1,0:T(2,128)}), f32[64,2,128]{2,1,0:T(2,128)S(1)}, u32[]{:S(2)}, u32[]{:S(2)}) %all-to-all-start) | async-done | bytes 65568 | tf_op jit(solution)/shard_map/all_to_all | solution.py:557
  47.1 0.4 slab.1
  47.5 21.6 %all_to_all.10 = f32[64,2,128]{2,1,0:T(2,128)S(1)} all-to-all(f32[64,2,128]{2,1,0:T(2,128)S(1)} %bitcast.18), channel_id=1, replica_groups=mesh['tm'=64,'net'=8] {'tm'}, dimensions={0} | all-to-all | bytes 131072 | tf_op jit(solution)/shard_map/all_to_all | solution.py:557
  69.1 3.3 %last.1 = f32[2048,128]{1,0:T(8,128)} custom-call(f32[2112,128]{1,0:T(8,128)S(1)} %get-tuple-element.16.f_ref, f32[136,128]{1,0:T(8,128)S(1)} %collective-permute-done.right_ref, f32[136,128]{1,0:T(8,128)S(1)} %collective-permute-done.1.left_ref, f32[2,192,128]{2,1,0:T(8,128)S(1)} %get-tuple-element.20.r1_ref, f32[2,24,128]{2,1,0:T(8,128)S(1)} %get-tuple-element.21.r2_ref, ...), custom_call_target="tpu_custom_call" | custom-call | tf_op jit(solution)/shard_map/last/pallas_call | solution.py:536
Async XLA Ops:
  1.4 5.1 %collective-permute-start = (f32[136,128]{1,0:T(8,128)S(1)}, f32[136,128]{1,0:T(8,128)S(1)}, u32[]{:S(2)}, u32[]{:S(2)}) collective-permute-start(f32[136,128]{1,0:T(8,128)S(1)} %get-tuple-element.17), channel_id=1, source_target_pairs={{1,0},{2,1},{3,2},{4,3},{5,4},{6,5},{7,6},{9,8},{10,9},{11,10},{12... | collective-permute-start | bytes 208904 | tf_op jit(solution)/shard_map/ppermute | solution.py:569
  3.5 5.6 %collective-permute-start.1 = (f32[136,128]{1,0:T(8,128)S(1)}, f32[136,128]{1,0:T(8,128)S(1)}, u32[]{:S(2)}, u32[]{:S(2)}) collective-permute-start(f32[136,128]{1,0:T(8,128)S(1)} %get-tuple-element.18), channel_id=1, source_target_pairs={{0,1},{1,2},{2,3},{3,4},{4,5},{5,6},{6,7},{8,9},{9,10},{10,11},{11... | collective-permute-start | bytes 208904 | tf_op jit(solution)/shard_map/ppermute | solution.py:568
  13.8 33.2 %all-to-all-start = ((f32[64,2,128]{2,1,0:T(2,128)}), f32[64,2,128]{2,1,0:T(2,128)S(1)}, u32[]{:S(2)}, u32[]{:S(2)}) async-start(f32[64,2,128]{2,1,0:T(2,128)} %bitcast.6), calls=%async_computation | async-start | bytes 131072 | tf_op jit(solution)/shard_map/all_to_all | solution.py:557
